TPU v7x, 32 devices: a whole 2x2x4 slice. The times are simulated.
32 devices in a mesh: pts: 16 (over z, x, core), cen: 2 (over y).
Axes of the slice: x: 2, y: 2, z: 4, core: 2. Of those that a mesh axis runs over, the one named last changes fastest.
Arguments:
- states: bfloat16 [8192, 512], P(('pts', 'cen')), may hold values from -48 to 48
- first_weight: bfloat16 [512, 1024], replicated, may hold values from -0.25 to 0.25
- first_bias: float32 [1024], replicated, may hold values from -4 to 4
- second_weight: bfloat16 [1024, 256], replicated, may hold values from -0.1875 to 0.1875
- centroids: bfloat16 [2, 4096, 256], P('cen'), may hold values from -3.59375 to 3.59375
Outputs:
- new_centroids: float32 [2, 4096, 256], P('cen', 'pts')
- sample_blended_penalty: float32 [8192], P(('pts', 'cen'))
All inputs are finite; a program needn't handle non-finite values.
Results may differ from a plain program's by a relative error of at most 0.0061.
Values may be sent and summed in bfloat16 or wider, within the bound.
A program may use at most 128 MiB of HBM per device.

v0:
```python
import math

import jax
import jax.numpy as jnp
from jax import lax
from jax.sharding import PartitionSpec as P

smoothing_scale = 16.0


def encode(states, first_weight, first_bias, second_weight):
    pre = jnp.dot(states, first_weight, preferred_element_type=jnp.float32) + first_bias
    hidden = jax.nn.gelu(pre).astype(jnp.bfloat16)
    return jnp.dot(hidden, second_weight, preferred_element_type=jnp.float32).astype(jnp.bfloat16)


def squares(rows):
    return jnp.sum(jnp.square(rows.astype(jnp.float32)), axis=1)


def tile_scores(rows, sample_length_squared, centers, center_length_squared):
    inner_pairing_matrix = lax.dot_general(
        rows, centers, (((1,), (1,)), ((), ())), preferred_element_type=jnp.float32
    )
    return (
        2.0 * inner_pairing_matrix - center_length_squared[None, :] - sample_length_squared[:, None]
    ) / smoothing_scale


def body(states, first_weight, first_bias, second_weight, centroids):
    codes = encode(states, first_weight, first_bias, second_weight)
    group = lax.all_gather(codes, "cen", axis=0, tiled=True)
    group_sq = squares(group)
    centers = centroids[0]
    count_centers, embedding_dimension = centers.shape
    center_block = math.gcd(count_centers, 512)
    center_tiles = centers.reshape(count_centers // center_block, center_block, embedding_dimension)
    center_length_squared = squares(centers)
    square_tiles = center_length_squared.reshape(count_centers // center_block, center_block)
    group_rows = group.shape[0]

    def local_pass(carry, pieces):
        running_maximum, running_sum = carry
        tile, tile_sq = pieces
        scores = tile_scores(group, group_sq, tile, tile_sq)
        peak_next = jnp.maximum(running_maximum, jnp.max(scores, axis=1))
        total_next = running_sum * jnp.exp(running_maximum - peak_next) + jnp.sum(
            jnp.exp(scores - peak_next[:, None]), axis=1
        )
        return ((peak_next, total_next), None)

    start_stats = (
        jnp.full((group_rows,), -jnp.inf, jnp.float32),
        jnp.zeros((group_rows,), jnp.float32),
    )
    (local_peak, local_total), _ = lax.scan(local_pass, start_stats, (center_tiles, square_tiles))
    running_maximum = lax.pmax(local_peak, "cen")
    running_sum = lax.psum(local_total * jnp.exp(local_peak - running_maximum), "cen")
    cluster_penalty_batch = -(smoothing_scale / embedding_dimension) * (
        running_maximum + jnp.log(running_sum)
    )
    own_rows = codes.shape[0]
    sample_blended_penalty = lax.dynamic_slice_in_dim(
        cluster_penalty_batch, lax.axis_index("cen") * own_rows, own_rows, 0
    )
    owned = count_centers // lax.axis_size("pts")
    owned_start = lax.axis_index("pts") * owned
    own_centers = lax.dynamic_slice_in_dim(centers, owned_start, owned, 0)
    normalizer = running_maximum + jnp.log(running_sum)
    every_code = lax.all_gather(group, "pts", axis=0, tiled=True)
    every_norm = lax.all_gather(normalizer, "pts", axis=0, tiled=True)
    own_sq = squares(own_centers)
    all_rows = every_code.shape[0]
    row_block = math.gcd(all_rows, 2048)
    tiles = all_rows // row_block

    def owner_pass(carry, pieces):
        weighted, counts = carry
        code_tile, norm_tile = pieces
        scores = tile_scores(code_tile, squares(code_tile), own_centers, own_sq)
        resp = jnp.exp(scores - norm_tile[:, None])
        counts = counts + jnp.sum(resp, axis=0)
        weighted = weighted + lax.dot_general(
            resp.astype(jnp.bfloat16),
            code_tile,
            (((0,), (0,)), ((), ())),
            preferred_element_type=jnp.float32,
        )
        return ((weighted, counts), None)

    start_sums = (
        jnp.zeros((owned, embedding_dimension), jnp.float32),
        jnp.zeros((owned,), jnp.float32),
    )
    (weighted, counts), _ = lax.scan(
        owner_pass,
        start_sums,
        (
            every_code.reshape(tiles, row_block, embedding_dimension),
            every_norm.reshape(tiles, row_block),
        ),
    )
    fresh = (weighted + own_centers.astype(jnp.float32)) / (counts + 1.0)[:, None]
    return (fresh[None], sample_blended_penalty)


def solution(mesh):
    placed = (P(("pts", "cen"), None), P(), P(), P(), P("cen", None, None))
    return jax.shard_map(
        body,
        mesh=mesh,
        in_specs=placed,
        out_specs=(P("cen", "pts", None), P(("pts", "cen"))),
        check_vma=False,
    )
```

profile of v0, /device:TPU:0, one launch (start us, length us, event | category | flops | bytes accessed | tf_op | source)
XLA Modules:
  0.0 102.2 jit_solution(7298496898274478168)
XLA Ops:
  7.2 0.0 copy-start
  7.2 0.0 copy-start.1
  7.2 0.0 all-gather.3.cloned.1.call-start
  7.2 1.2 %copy-done = bf16[512,1024]{1,0:T(8,128)(2,1)S(1)} copy-done((bf16[512,1024]{1,0:T(8,128)(2,1)S(1)}, bf16[512,1024]{1,0:T(8,128)(2,1)}, u32[]{:S(2)}) %copy-start) | copy-done | bytes 1048600
  8.4 1.9 %convolution_convert_fusion = bf16[256,256]{1,0:T(8,128)(2,1)S(1)} fusion(bf16[1024,256]{1,0:T(8,128)(2,1)} %param.12, bf16[256,512]{1,0:T(8,128)(2,1)} %param.9, bf16[512,1024]{1,0:T(8,128)(2,1)S(1)} %copy-done, f32[1024]{0:T(1024)} %param.11), kind=kOutput, calls=%fused_computation.32 | convolution fusion | flops 405340160 | bytes 1970176 | tf_op jit(solution)/shard_map/dot_general | solution.py:14
  10.3 7.2 %all_gather.9 = bf16[512,256]{1,0:T(8,128)(2,1)} all-gather(bf16[256,256]{1,0:T(8,128)(2,1)S(1)} %convolution_convert_fusion), channel_id=1, replica_groups=mesh['pts'=16,'cen'=2] {'cen'}, dimensions={0}, use_global_device_ids=true | all-gather | bytes 393216 | tf_op jit(solution)/shard_map/all_gather | solution.py:32
  17.6 0.0 all-gather.3.cloned.1.call-update
  17.6 1.1 %multiply_reduce_fusion.2 = f32[512]{0:T(512)S(1)} fusion(bf16[512,256]{1,0:T(8,128)(2,1)} %all_gather.9), kind=kLoop, calls=%fused_computation.41 | loop fusion | flops 392704 | bytes 264192 | tf_op jit(solution)/shard_map/reduce_sum | solution.py:18
  18.7 0.0 copy-done.1
  18.7 0.6 multiply_reduce_fusion.1
  19.4 12.8 %while.26 = (s32[]{:T(128)}, f32[512]{0:T(512)S(1)}, f32[512]{0:T(512)S(1)}, bf16[8,512,256]{2,1,0:T(8,128)(2,1)S(1)}, bf16[512,256]{1,0:T(8,128)(2,1)}, /*index...) while((s32[]{:T(128)}, f32[512]{0:T(512)S(1)}, f32[512]{0:T(512)S(1)}, ...), condition=%wide.region_5.6_spmd.clone, body=%wide.region_2.5_spmd.clone.sunk | while | flops 136055296 | bytes 2656376 | solution.py:56
  19.4 1.3 %fusion.55 = (f32[512]{0:T(512)S(1)}, f32[512,512]{1,0:T(8,128)S(1)}) fusion(f32[512]{0:T(512)S(1)} %get-tuple-element.286, f32[512]{0:T(512)S(1)} %bitcast.51, bf16[512,256]{1,0:T(8,128)(2,1)} %get-tuple-element.284, bf16[8,512,256]{2,1,0:T(8,128)(2,1)S(1)} %get-tuple-element.283, s32[]{:T(128)S(6)} %copy.10), kind=kOutput, calls=%fused_computation.61.clone.1 | convolution fusion | flops 135527936 | bytes 1579012 | tf_op jit(solution)/shard_map/while/body/eval_jaxpr/dot_general | solution.py:22
  20.8 0.2 exponential_reduce_fusion.2
  21.0 1.3 %fusion.55 = (f32[512]{0:T(512)S(1)}, f32[512,512]{1,0:T(8,128)S(1)}) fusion(f32[512]{0:T(512)S(1)} %get-tuple-element.286, f32[512]{0:T(512)S(1)} %bitcast.51, bf16[512,256]{1,0:T(8,128)(2,1)} %get-tuple-element.284, bf16[8,512,256]{2,1,0:T(8,128)(2,1)S(1)} %get-tuple-element.283, s32[]{:T(128)S(6)} %copy.10), kind=kOutput, calls=%fused_computation.61.clone.1 | convolution fusion | flops 135527936 | bytes 1579012 | tf_op jit(solution)/shard_map/while/body/eval_jaxpr/dot_general | solution.py:22
  22.4 0.2 exponential_reduce_fusion.2
  22.6 1.3 %fusion.55 = (f32[512]{0:T(512)S(1)}, f32[512,512]{1,0:T(8,128)S(1)}) fusion(f32[512]{0:T(512)S(1)} %get-tuple-element.286, f32[512]{0:T(512)S(1)} %bitcast.51, bf16[512,256]{1,0:T(8,128)(2,1)} %get-tuple-element.284, bf16[8,512,256]{2,1,0:T(8,128)(2,1)S(1)} %get-tuple-element.283, s32[]{:T(128)S(6)} %copy.10), kind=kOutput, calls=%fused_computation.61.clone.1 | convolution fusion | flops 135527936 | bytes 1579012 | tf_op jit(solution)/shard_map/while/body/eval_jaxpr/dot_general | solution.py:22
  24.0 0.2 exponential_reduce_fusion.2
  24.2 1.3 %fusion.55 = (f32[512]{0:T(512)S(1)}, f32[512,512]{1,0:T(8,128)S(1)}) fusion(f32[512]{0:T(512)S(1)} %get-tuple-element.286, f32[512]{0:T(512)S(1)} %bitcast.51, bf16[512,256]{1,0:T(8,128)(2,1)} %get-tuple-element.284, bf16[8,512,256]{2,1,0:T(8,128)(2,1)S(1)} %get-tuple-element.283, s32[]{:T(128)S(6)} %copy.10), kind=kOutput, calls=%fused_computation.61.clone.1 | convolution fusion | flops 135527936 | bytes 1579012 | tf_op jit(solution)/shard_map/while/body/eval_jaxpr/dot_general | solution.py:22
  25.6 0.2 exponential_reduce_fusion.2
  25.8 1.3 %fusion.55 = (f32[512]{0:T(512)S(1)}, f32[512,512]{1,0:T(8,128)S(1)}) fusion(f32[512]{0:T(512)S(1)} %get-tuple-element.286, f32[512]{0:T(512)S(1)} %bitcast.51, bf16[512,256]{1,0:T(8,128)(2,1)} %get-tuple-element.284, bf16[8,512,256]{2,1,0:T(8,128)(2,1)S(1)} %get-tuple-element.283, s32[]{:T(128)S(6)} %copy.10), kind=kOutput, calls=%fused_computation.61.clone.1 | convolution fusion | flops 135527936 | bytes 1579012 | tf_op jit(solution)/shard_map/while/body/eval_jaxpr/dot_general | solution.py:22
  27.2 0.2 exponential_reduce_fusion.2
  27.4 1.4 %fusion.55 = (f32[512]{0:T(512)S(1)}, f32[512,512]{1,0:T(8,128)S(1)}) fusion(f32[512]{0:T(512)S(1)} %get-tuple-element.286, f32[512]{0:T(512)S(1)} %bitcast.51, bf16[512,256]{1,0:T(8,128)(2,1)} %get-tuple-element.284, bf16[8,512,256]{2,1,0:T(8,128)(2,1)S(1)} %get-tuple-element.283, s32[]{:T(128)S(6)} %copy.10), kind=kOutput, calls=%fused_computation.61.clone.1 | convolution fusion | flops 135527936 | bytes 1579012 | tf_op jit(solution)/shard_map/while/body/eval_jaxpr/dot_general | solution.py:22
  28.8 0.2 exponential_reduce_fusion.2
  29.0 1.3 %fusion.55 = (f32[512]{0:T(512)S(1)}, f32[512,512]{1,0:T(8,128)S(1)}) fusion(f32[512]{0:T(512)S(1)} %get-tuple-element.286, f32[512]{0:T(512)S(1)} %bitcast.51, bf16[512,256]{1,0:T(8,128)(2,1)} %get-tuple-element.284, bf16[8,512,256]{2,1,0:T(8,128)(2,1)S(1)} %get-tuple-element.283, s32[]{:T(128)S(6)} %copy.10), kind=kOutput, calls=%fused_computation.61.clone.1 | convolution fusion | flops 135527936 | bytes 1579012 | tf_op jit(solution)/shard_map/while/body/eval_jaxpr/dot_general | solution.py:22
  30.4 0.2 exponential_reduce_fusion.2
  30.6 1.3 %fusion.55 = (f32[512]{0:T(512)S(1)}, f32[512,512]{1,0:T(8,128)S(1)}) fusion(f32[512]{0:T(512)S(1)} %get-tuple-element.286, f32[512]{0:T(512)S(1)} %bitcast.51, bf16[512,256]{1,0:T(8,128)(2,1)} %get-tuple-element.284, bf16[8,512,256]{2,1,0:T(8,128)(2,1)S(1)} %get-tuple-element.283, s32[]{:T(128)S(6)} %copy.10), kind=kOutput, calls=%fused_computation.61.clone.1 | convolution fusion | flops 135527936 | bytes 1579012 | tf_op jit(solution)/shard_map/while/body/eval_jaxpr/dot_general | solution.py:22
  32.0 0.2 exponential_reduce_fusion.2
  32.2 4.9 %pmax.7 = f32[512]{0:T(512)S(1)} all-reduce(f32[512]{0:T(512)S(1)} %get-tuple-element.78), channel_id=1, replica_groups=mesh['pts'=16,'cen'=2] {'cen'}, use_global_device_ids=true, to_apply=%region_6.7 | all-reduce | flops 512 | bytes 4096 | tf_op jit(solution)/shard_map/pmax | solution.py:57
  37.2 4.9 %psum.7 = f32[512]{0:T(512)S(1)} all-reduce(f32[512]{0:T(512)S(1)} %exponential_multiply_fusion), channel_id=1, replica_groups=mesh['pts'=16,'cen'=2] {'cen'}, use_global_device_ids=true, to_apply=%region_7.8 | all-reduce | flops 512 | bytes 4096 | tf_op jit(solution)/shard_map/psum | solution.py:58
  42.1 22.6 %all-gather = f32[16,1,512]{2,1,0:T(1,128)S(1)} all-gather(f32[1,1,512]{2,1,0:T(1,128)S(1)} %bitcast.52), channel_id=1, replica_groups=mesh['pts'=16,'cen'=2] {'pts'}, dimensions={0}, use_global_device_ids=true | all-gather | bytes 34816 | tf_op jit(solution)/shard_map/all_gather | solution.py:71
  64.7 0.1 reduce.3
  64.7 0.6 reshape.26
  65.4 0.6 dynamic_slice.26
  66.0 0.1 fusion.32
  66.1 3.8 %all-gather.3.cloned.1.call-done = bf16[8192,256]{1,0:T(8,128)(2,1)} async-done(((bf16[512,256]{1,0:T(8,128)(2,1)}), bf16[8192,256]{1,0:T(8,128)(2,1)}) %all-gather.3.cloned.1.call-update) | async-done | bytes 4194320 | tf_op jit(solution)/shard_map/all_gather | solution.py:70
  69.9 24.7 %while.27 = (s32[]{:T(128)}, f32[256,256]{1,0:T(8,128)S(1)}, f32[256]{0:T(256)S(1)}, bf16[4,2048,256]{2,1,0:T(8,128)(2,1)}, bf16[256,256]{1,0:T(8,128)(2,1)S(1)}...) while((s32[]{:T(128)}, f32[256,256]{1,0:T(8,128)S(1)}, ...), condition=%wide.region_12.13_spmd.clone, body=%wide.region_9.12_spmd.clone.sunk | while | flops 542243072 | bytes 5944448 | solution.py:95
  69.9 0.8 constant_dynamic-slice_fusion.5
  70.7 1.6 %multiply_reduce_fusion.4 = f32[2048]{0:T(1024)S(1)} fusion(bf16[4,2048,256]{2,1,0:T(8,128)(2,1)} %get-tuple-element.310, s32[]{:T(128)S(6)} %copy.19), kind=kLoop, calls=%fused_computation.18.clone.1 | loop fusion | flops 1570816 | bytes 1056772 | tf_op jit(solution)/shard_map/while/body/eval_jaxpr/reduce_sum | solution.py:18
  72.2 2.0 %fusion.60 = (f32[256]{0:T(256)S(1)}, bf16[2048,256]{1,0:T(8,128)(2,1)S(1)}) fusion(f32[2048]{0:T(1024)S(1)} %bitcast.50, f32[2048]{0:T(1024)S(1)} %multiply_reduce_fusion.4, f32[256]{0:T(256)S(1)} %get-tuple-element.312, bf16[256,256]{1,0:T(8,128)(2,1)S(1)} %get-tuple-element.311, bf16[4,2048,256]{2,1,0:T(8,128)(2,1)} %get-tuple-element.310, ...), kind=kOutput, calls=%fused_computation.62.clone.1 | convolution fusion | flops 272105216 | bytes 2246660 | tf_op jit(solution)/shard_map/while/body/eval_jaxpr/dot_general | solution.py:22
  74.3 1.8 %convolution_add_fusion.3 = f32[256,256]{1,0:T(8,128)S(1)} fusion(bf16[2048,256]{1,0:T(8,128)(2,1)S(1)} %get-tuple-element.260, bf16[4,2048,256]{2,1,0:T(8,128)(2,1)} %get-tuple-element.310, s32[]{:T(128)S(6)} %copy.19, f32[256,256]{1,0:T(8,128)S(1)} %get-tuple-element.299, pred[]{:T(512)S(6)} %compare.7), kind=kOutput, calls=%fused_computation.19.clone.1 | convolution fusion | flops 268566528 | bytes 2621445 | tf_op jit(solution)/shard_map/while/body/eval_jaxpr/dot_general | solution.py:83
  76.1 0.8 constant_dynamic-slice_fusion.5
  76.8 1.6 %multiply_reduce_fusion.4 = f32[2048]{0:T(1024)S(1)} fusion(bf16[4,2048,256]{2,1,0:T(8,128)(2,1)} %get-tuple-element.310, s32[]{:T(128)S(6)} %copy.19), kind=kLoop, calls=%fused_computation.18.clone.1 | loop fusion | flops 1570816 | bytes 1056772 | tf_op jit(solution)/shard_map/while/body/eval_jaxpr/reduce_sum | solution.py:18
  78.4 2.0 %fusion.60 = (f32[256]{0:T(256)S(1)}, bf16[2048,256]{1,0:T(8,128)(2,1)S(1)}) fusion(f32[2048]{0:T(1024)S(1)} %bitcast.50, f32[2048]{0:T(1024)S(1)} %multiply_reduce_fusion.4, f32[256]{0:T(256)S(1)} %get-tuple-element.312, bf16[256,256]{1,0:T(8,128)(2,1)S(1)} %get-tuple-element.311, bf16[4,2048,256]{2,1,0:T(8,128)(2,1)} %get-tuple-element.310, ...), kind=kOutput, calls=%fused_computation.62.clone.1 | convolution fusion | flops 272105216 | bytes 2246660 | tf_op jit(solution)/shard_map/while/body/eval_jaxpr/dot_general | solution.py:22
  80.4 1.8 %convolution_add_fusion.3 = f32[256,256]{1,0:T(8,128)S(1)} fusion(bf16[2048,256]{1,0:T(8,128)(2,1)S(1)} %get-tuple-element.260, bf16[4,2048,256]{2,1,0:T(8,128)(2,1)} %get-tuple-element.310, s32[]{:T(128)S(6)} %copy.19, f32[256,256]{1,0:T(8,128)S(1)} %get-tuple-element.299, pred[]{:T(512)S(6)} %compare.7), kind=kOutput, calls=%fused_computation.19.clone.1 | convolution fusion | flops 268566528 | bytes 2621445 | tf_op jit(solution)/shard_map/while/body/eval_jaxpr/dot_general | solution.py:83
  82.2 0.8 constant_dynamic-slice_fusion.5
  83.0 1.6 %multiply_reduce_fusion.4 = f32[2048]{0:T(1024)S(1)} fusion(bf16[4,2048,256]{2,1,0:T(8,128)(2,1)} %get-tuple-element.310, s32[]{:T(128)S(6)} %copy.19), kind=kLoop, calls=%fused_computation.18.clone.1 | loop fusion | flops 1570816 | bytes 1056772 | tf_op jit(solution)/shard_map/while/body/eval_jaxpr/reduce_sum | solution.py:18
  84.6 2.0 %fusion.60 = (f32[256]{0:T(256)S(1)}, bf16[2048,256]{1,0:T(8,128)(2,1)S(1)}) fusion(f32[2048]{0:T(1024)S(1)} %bitcast.50, f32[2048]{0:T(1024)S(1)} %multiply_reduce_fusion.4, f32[256]{0:T(256)S(1)} %get-tuple-element.312, bf16[256,256]{1,0:T(8,128)(2,1)S(1)} %get-tuple-element.311, bf16[4,2048,256]{2,1,0:T(8,128)(2,1)} %get-tuple-element.310, ...), kind=kOutput, calls=%fused_computation.62.clone.1 | convolution fusion | flops 272105216 | bytes 2246660 | tf_op jit(solution)/shard_map/while/body/eval_jaxpr/dot_general | solution.py:22
  86.6 1.8 %convolution_add_fusion.3 = f32[256,256]{1,0:T(8,128)S(1)} fusion(bf16[2048,256]{1,0:T(8,128)(2,1)S(1)} %get-tuple-element.260, bf16[4,2048,256]{2,1,0:T(8,128)(2,1)} %get-tuple-element.310, s32[]{:T(128)S(6)} %copy.19, f32[256,256]{1,0:T(8,128)S(1)} %get-tuple-element.299, pred[]{:T(512)S(6)} %compare.7), kind=kOutput, calls=%fused_computation.19.clone.1 | convolution fusion | flops 268566528 | bytes 2621445 | tf_op jit(solution)/shard_map/while/body/eval_jaxpr/dot_general | solution.py:83
  88.4 0.8 constant_dynamic-slice_fusion.5
  89.2 1.6 %multiply_reduce_fusion.4 = f32[2048]{0:T(1024)S(1)} fusion(bf16[4,2048,256]{2,1,0:T(8,128)(2,1)} %get-tuple-element.310, s32[]{:T(128)S(6)} %copy.19), kind=kLoop, calls=%fused_computation.18.clone.1 | loop fusion | flops 1570816 | bytes 1056772 | tf_op jit(solution)/shard_map/while/body/eval_jaxpr/reduce_sum | solution.py:18
  90.8 2.0 %fusion.60 = (f32[256]{0:T(256)S(1)}, bf16[2048,256]{1,0:T(8,128)(2,1)S(1)}) fusion(f32[2048]{0:T(1024)S(1)} %bitcast.50, f32[2048]{0:T(1024)S(1)} %multiply_reduce_fusion.4, f32[256]{0:T(256)S(1)} %get-tuple-element.312, bf16[256,256]{1,0:T(8,128)(2,1)S(1)} %get-tuple-element.311, bf16[4,2048,256]{2,1,0:T(8,128)(2,1)} %get-tuple-element.310, ...), kind=kOutput, calls=%fused_computation.62.clone.1 | convolution fusion | flops 272105216 | bytes 2246660 | tf_op jit(solution)/shard_map/while/body/eval_jaxpr/dot_general | solution.py:22
  92.8 1.8 %convolution_add_fusion.3 = f32[256,256]{1,0:T(8,128)S(1)} fusion(bf16[2048,256]{1,0:T(8,128)(2,1)S(1)} %get-tuple-element.260, bf16[4,2048,256]{2,1,0:T(8,128)(2,1)} %get-tuple-element.310, s32[]{:T(128)S(6)} %copy.19, f32[256,256]{1,0:T(8,128)S(1)} %get-tuple-element.299, pred[]{:T(512)S(6)} %compare.7), kind=kOutput, calls=%fused_computation.19.clone.1 | convolution fusion | flops 268566528 | bytes 2621445 | tf_op jit(solution)/shard_map/while/body/eval_jaxpr/dot_general | solution.py:83
  94.6 0.8 fusion.34
  (44 shorter events, 0.4 us)
Async XLA Ops:
  7.2 1.2 %copy-start = (bf16[512,1024]{1,0:T(8,128)(2,1)S(1)}, bf16[512,1024]{1,0:T(8,128)(2,1)}, u32[]{:S(2)}) copy-start(bf16[512,1024]{1,0:T(8,128)(2,1)} %param.10) | copy-start | bytes 3145732
  7.2 11.6 %copy-start.1 = (bf16[1,4096,256]{2,1,0:T(8,128)(2,1)S(1)}, bf16[1,4096,256]{2,1,0:T(8,128)(2,1)}, u32[]{:S(2)}) copy-start(bf16[1,4096,256]{2,1,0:T(8,128)(2,1)} %param.13) | copy-start | bytes 6291460
  7.2 62.7 %all-gather.3.cloned.1.call-start = ((), (), s32[]{:S(2)}) async-start(), calls=%async_computation | async-start | bytes 4456448 | tf_op jit(solution)/shard_map/all_gather | solution.py:70
Sparse Core Ops, SparseCore 0:
  17.7 52.1 all-gather.2
where the time goes:
time: 103 us; the launch traced here: 102 us
  blocking collectives  39.7 us (39%)
  matrix products  27.7 us (27%)
  between operations  14.2 us (14%)
  other arithmetic  10.8 us (10%)
  local copies, waits for them, and re-layouts  5.62 us (5%)
  waiting for transfers between devices  3.79 us (4%)
    all_gather x1, blocking collectives, body(): every_norm = lax.all_gather(normalizer, 'pts', axis=0, tiled=True)  22.6 us
    dot_general x12, matrix products, tile_scores(): lax.dot_general(rows, centers, (((1,), (1,)), ((), ())), preferred_elemen...  18.8 us
    reduce_sum x7, other arithmetic, squares(): return jnp.sum(jnp.square(rows.astype(jnp.float32)), axis=1)  8.11 us
    all_gather x1, blocking collectives, body(): group = lax.all_gather(codes, 'cen', axis=0, tiled=True)  7.25 us
    dot_general x4, matrix products, owner_pass(): lax.dot_general(resp.astype(jnp.bfloat16), code_tile, (((0,), (0,)), ((),...  7.04 us
    pmax x1, blocking collectives, body(): running_maximum = lax.pmax(local_peak, 'cen')  4.93 us
    psum x1, blocking collectives, body(): lax.psum(local_total * jnp.exp(local_peak - running_maximum), 'cen')  4.92 us
    all_gather x1, waiting for transfers between devices, body(): every_code = lax.all_gather(group, 'pts', axis=0, tiled=True)  3.77 us
  transfers between devices with their start and end apart: 1, of which 1 were waited for; matrix products, arithmetic and copies ran while one was open for 15% of the time, Pallas kernels for 0%

commit v1 on v0

v1 whole, which is shorter than its diff:
```python
import functools

import jax
import jax.numpy as jnp
from jax import lax
from jax.experimental import pallas as pl
from jax.experimental.pallas import tpu as pltpu
from jax.sharding import PartitionSpec as P

smoothing_scale = 16.0
MESH = pl.DeviceIdType.MESH
NT = (((1,), (1,)), ((), ()))


def encode(states, first_weight, first_bias, second_weight):
    pre = jnp.dot(states, first_weight, preferred_element_type=jnp.float32) + first_bias
    hidden = jax.nn.gelu(pre).astype(jnp.bfloat16)
    return jnp.dot(hidden, second_weight, preferred_element_type=jnp.float32).astype(jnp.bfloat16)


def scaled_squares(rows):
    wide = rows.astype(jnp.float32)
    return jnp.sum(wide * wide, axis=1, keepdims=True) / smoothing_scale


def kernel(
    n_pts, n_cen, codes_ref, cen_ref, out_ref, pen_ref,
    allc, stat, norm, weighted, counts, own_sq,
    recv, half, stat_recv, norm_recv,
    send_z, send_x, send_c, send_core, send_hx, send_hc, send_stat, send_norm, own_sem,
):
    n, width = codes_ref.shape
    n_z = n_pts // 4
    p, c = lax.axis_index("pts"), lax.axis_index("cen")
    core, x, z = lax.rem(p, 2), lax.rem(p // 2, 2), p // 4

    def pts_of(zi, xi, ki):
        return (zi * 2 + xi) * 2 + ki

    def z_at(k):
        return lax.rem(z + k, n_z)

    def c_at(j):
        return lax.rem(c + j, n_cen)

    def block(zi, xi, ki, ci):
        return pts_of(zi, xi, ki) * n_cen + ci

    x_peer = (pts_of(z, 1 - x, core), c)
    core_peer = (pts_of(z, x, 1 - core), c)
    mine = block(z, x, core, c)

    def remote(src, dst, send_sem, recv_sem, peer):
        return pltpu.make_async_remote_copy(
            src_ref=src, dst_ref=dst, send_sem=send_sem, recv_sem=recv_sem,
            device_id=peer, device_id_type=MESH,
        )

    sent = []

    def push(copy):
        copy.start()
        sent.append(copy)

    def whole(b, send_sem, peer, src=None):
        push(remote(allc.at[b] if src is None else src, allc.at[b], send_sem, recv.at[b], peer))

    def part(b, h, send_sem, peer):
        rows = pl.ds(h * (n // 2), n // 2)
        push(remote(allc.at[b, rows], allc.at[b, rows], send_sem, half.at[b, h], peer))

    def arrived(b):
        remote(allc.at[b], allc.at[b], own_sem, recv.at[b], core_peer).wait_recv()

    def part_arrived(b, h):
        rows = pl.ds(h * (n // 2), n // 2)
        remote(allc.at[b, rows], allc.at[b, rows], own_sem, half.at[b, h], core_peer).wait_recv()

    barrier = pltpu.get_barrier_semaphore()
    for k in range(1, n_pts):
        pl.semaphore_signal(
            barrier, inc=1, device_id=(lax.rem(p + k, n_pts), c), device_id_type=MESH
        )
    for j in range(1, n_cen):
        pl.semaphore_signal(barrier, inc=1, device_id=(p, c_at(j)), device_id_type=MESH)
    pl.semaphore_wait(barrier, n_pts - 1 + n_cen - 1)

    own = pltpu.make_async_copy(codes_ref, allc.at[mine], own_sem)
    own.start()
    for j in range(1, n_cen):
        whole(mine, send_c.at[0, j], (p, c_at(j)), codes_ref)
    for k in range(1, n_z):
        whole(mine, send_z.at[k], (pts_of(z_at(k), x, core), c), codes_ref)
    whole(mine, send_x.at[0], x_peer, codes_ref)
    whole(mine, send_core.at[0, 0, 0], core_peer, codes_ref)
    own.wait()

    owned = out_ref.shape[0]
    own_rows = pl.ds(pl.multiple_of(p * owned, owned), owned)
    own_sq[...] = scaled_squares(cen_ref[0, own_rows, :])

    for k in range(1, n_z):
        b = block(z_at(k), x, core, c)
        arrived(b)
        whole(b, send_x.at[k], x_peer)
        for j in range(1, n_cen):
            whole(b, send_c.at[k, j], (p, c_at(j)))
        whole(b, send_core.at[k, 0, 0], core_peer)

    def from_cen(k):
        for j in range(1, n_cen):
            b = block(z_at(k), x, core, c_at(j))
            arrived(b)
            part(b, 1, send_hx.at[k, j], x_peer)
            whole(b, send_core.at[k, 0, j], core_peer)

    from_cen(0)

    tile = min(256, cen_ref.shape[1])
    group_rows = n * n_cen
    group = pl.ds(p * n_cen, n_cen)

    def stats_step(i, carry):
        peak, total = carry
        centers = cen_ref[0, pl.ds(pl.multiple_of(i * tile, tile), tile), :]
        rows = allc[group].reshape(group_rows, width)
        scores = lax.dot_general(centers, rows, NT, preferred_element_type=jnp.float32)
        scores = scores * (2.0 / smoothing_scale) - scaled_squares(centers)
        peak_next = jnp.maximum(peak, jnp.max(scores, axis=0, keepdims=True))
        total_next = total * jnp.exp(peak - peak_next) + jnp.sum(
            jnp.exp(scores - peak_next), axis=0, keepdims=True
        )
        return peak_next, total_next

    peak, total = lax.fori_loop(
        0,
        cen_ref.shape[1] // tile,
        stats_step,
        (
            jnp.full((1, group_rows), -jnp.inf, jnp.float32),
            jnp.zeros((1, group_rows), jnp.float32),
        ),
    )
    first = lax.broadcasted_iota(jnp.int32, (8, n), 0) == 0
    for j in range(n_cen):
        cols = slice(j * n, (j + 1) * n)
        stat[c, j] = jnp.where(first, peak[:, cols], total[:, cols])
    for j in range(1, n_cen):
        push(remote(stat.at[c], stat.at[c], send_stat.at[j], stat_recv.at[c], (p, c_at(j))))

    for k in range(n_z):
        b = block(z_at(k), 1 - x, core, c)
        arrived(b)
        for j in range(1, n_cen):
            part(b, 0, send_hc.at[k, j], (p, c_at(j)))
        whole(b, send_core.at[k, 1, 0], core_peer)
        if k > 0:
            from_cen(k)

    for j in range(1, n_cen):
        s = c_at(j)
        remote(stat.at[s], stat.at[s], own_sem, stat_recv.at[s], (p, s)).wait_recv()
    for j in range(n_cen):
        top = stat[0, j][0:1, :]
        for s in range(1, n_cen):
            top = jnp.maximum(top, stat[s, j][0:1, :])
        mass = jnp.zeros_like(top)
        for s in range(n_cen):
            piece = stat[s, j]
            mass = mass + piece[1:2, :] * jnp.exp(piece[0:1, :] - top)
        norm[p, j] = jnp.broadcast_to(top + jnp.log(mass), (8, n))
    for k in range(1, n_pts):
        push(
            remote(
                norm.at[p], norm.at[p], send_norm.at[k], norm_recv.at[p],
                (lax.rem(p + k, n_pts), c),
            )
        )
    wide = codes_ref[...].astype(jnp.float32)
    lengths = lax.dot_general(
        jnp.ones((8, width), jnp.float32), wide * wide, NT,
        preferred_element_type=jnp.float32, precision=lax.Precision.HIGHEST,
    )
    pen_ref[...] = (-(smoothing_scale / width)) * (
        norm[p, c][0:1, :] - lengths[0:1, :] / smoothing_scale
    )

    for k in range(n_z):
        for j in range(1, n_cen):
            b = block(z_at(k), 1 - x, core, c_at(j))
            part_arrived(b, 0)
            part_arrived(b, 1)
            whole(b, send_core.at[k, 1, j], core_peer)

    for k in range(1, n_pts):
        s = lax.rem(p + k, n_pts)
        remote(norm.at[s], norm.at[s], own_sem, norm_recv.at[s], (s, c)).wait_recv()

    weighted[...] = jnp.zeros_like(weighted)
    counts[...] = jnp.zeros_like(counts)

    def consume(zi, xi, ki, ci):
        rows = allc[block(zi, xi, ki, ci)]
        scores = lax.dot_general(
            cen_ref[0, own_rows, :], rows, NT, preferred_element_type=jnp.float32
        )
        shift = norm[pts_of(zi, xi, ki), ci][0:1, :]
        resp = jnp.exp(scores * (2.0 / smoothing_scale) - own_sq[...] - shift)
        lanes = resp[:, 0:128]
        for q in range(1, n // 128):
            lanes = lanes + resp[:, q * 128:(q + 1) * 128]
        counts[...] += lanes
        weighted[...] += jnp.dot(
            resp.astype(jnp.bfloat16), rows, preferred_element_type=jnp.float32
        )

    def same_core(i, _):
        consume(i // (2 * n_cen), lax.rem(i // n_cen, 2), core, lax.rem(i, n_cen))
        return 0

    def other_core(i, _):
        zi, xi, ci = i // (2 * n_cen), lax.rem(i // n_cen, 2), lax.rem(i, n_cen)
        arrived(block(zi, xi, 1 - core, ci))
        consume(zi, xi, 1 - core, ci)
        return 0

    lax.fori_loop(0, n_z * 2 * n_cen, same_core, 0)
    lax.fori_loop(0, n_z * 2 * n_cen, other_core, 0)

    tally = jnp.sum(counts[...], axis=1, keepdims=True)
    out_ref[...] = (weighted[...] + cen_ref[0, own_rows, :].astype(jnp.float32)) / (tally + 1.0)
    for copy in sent:
        copy.wait_send()


def body(n_pts, n_cen, states, first_weight, first_bias, second_weight, centroids):
    codes = encode(states, first_weight, first_bias, second_weight)
    n, width = codes.shape
    owned = centroids.shape[1] // n_pts
    n_z = n_pts // 4
    dma = pltpu.SemaphoreType.DMA
    fresh, penalty = pl.pallas_call(
        functools.partial(kernel, n_pts, n_cen),
        out_shape=(
            jax.ShapeDtypeStruct((owned, width), jnp.float32),
            jax.ShapeDtypeStruct((1, n), jnp.float32),
        ),
        in_specs=[pl.BlockSpec(memory_space=pltpu.VMEM)] * 2,
        out_specs=(pl.BlockSpec(memory_space=pltpu.VMEM),) * 2,
        scratch_shapes=[
            pltpu.VMEM((n_pts * n_cen, n, width), jnp.bfloat16),
            pltpu.VMEM((n_cen, n_cen, 8, n), jnp.float32),
            pltpu.VMEM((n_pts, n_cen, 8, n), jnp.float32),
            pltpu.VMEM((owned, width), jnp.float32),
            pltpu.VMEM((owned, 128), jnp.float32),
            pltpu.VMEM((owned, 1), jnp.float32),
            dma((n_pts * n_cen,)),
            dma((n_pts * n_cen, 2)),
            dma((n_cen,)),
            dma((n_pts,)),
            dma((n_z,)),
            dma((n_z,)),
            dma((n_z, n_cen)),
            dma((n_z, 2, n_cen)),
            dma((n_z, n_cen)),
            dma((n_z, n_cen)),
            dma((n_cen,)),
            dma((n_pts,)),
            dma,
        ],
        compiler_params=pltpu.CompilerParams(
            collective_id=0, has_side_effects=True, vmem_limit_bytes=60 * 1024 * 1024
        ),
    )(codes, centroids)
    return (fresh[None], penalty.reshape(n))


def solution(mesh):
    placed = (P(("pts", "cen"), None), P(), P(), P(), P("cen", None, None))
    return jax.shard_map(
        functools.partial(body, mesh.shape["pts"], mesh.shape["cen"]),
        mesh=mesh,
        in_specs=placed,
        out_specs=(P("cen", "pts", None), P(("pts", "cen"))),
        check_vma=False,
    )
```

time: 103 us -> 59.1 us (0.57)
  the two profiles are of different devices: /device:TPU:0 before, /device:TPU:13 now
where the time goes in v1:
time: 59.1 us; the launch traced here: 58.9 us
  Pallas kernels  51.6 us (87%)
  local copies, waits for them, and re-layouts  4.12 us (7%)
  matrix products  2.56 us (4%)
  between operations  0.65 us (1%)
    pallas_call x1, Pallas kernels, body(): pl.pallas_call(functools.partial(kernel, n_pts, n_cen), out_shape=(jax.Sh...  51.6 us
    unnamed x4, local copies, waits for them, and re-layouts  4.12 us
    dot_general x1, matrix products, encode(): jnp.dot(hidden, second_weight, preferred_element_type=jnp.float32)  2.56 us

profile of v1, /device:TPU:13, one launch (start us, length us, event | category | flops | bytes accessed | tf_op | source)
XLA Modules:
  0.0 58.9 jit_solution(11408534390858536110)
XLA Ops:
  0.6 0.0 copy-start
  0.6 1.2 %copy-done = bf16[512,1024]{1,0:T(8,128)(2,1)S(1)} copy-done((bf16[512,1024]{1,0:T(8,128)(2,1)S(1)}, bf16[512,1024]{1,0:T(8,128)(2,1)}, u32[]{:S(2)}) %copy-start) | copy-done | bytes 1048600
  1.9 2.6 %convolution_convert_fusion.codes_ref = bf16[256,256]{1,0:T(8,128)(2,1)} fusion(bf16[1024,256]{1,0:T(8,128)(2,1)} %param.8, bf16[256,512]{1,0:T(8,128)(2,1)} %param.5, bf16[512,1024]{1,0:T(8,128)(2,1)S(1)} %copy-done, f32[1024]{0:T(1024)} %param.7), kind=kOutput, calls=%fused_computation.2 | convolution fusion | flops 405340160 | bytes 1970176 | tf_op jit(solution)/shard_map/dot_general | solution.py:18
  4.4 51.6 %shard_map.68 = (f32[256,256]{1,0:T(8,128)}, f32[1,256]{1,0:T(1,128)}) custom-call(bf16[256,256]{1,0:T(8,128)(2,1)} %convolution_convert_fusion.codes_ref, bf16[1,4096,256]{2,1,0:T(8,128)(2,1)} %cen_ref.1), custom_call_target="tpu_custom_call" | custom-call | tf_op jit(solution)/shard_map/pallas_call | solution.py:242
  56.0 1.7 %copy.9 = f32[1,256,256]{2,1,0:T(8,128)} copy(f32[1,256,256]{2,1,0:T(8,128)} %bitcast.5) | data formatting | bytes 524288
  57.7 1.2 %copy.10 = f32[256]{0:T(256)} copy(f32[256]{0:T(256)} %bitcast.6) | data formatting | bytes 2048
Async XLA Ops:
  0.6 1.2 %copy-start = (bf16[512,1024]{1,0:T(8,128)(2,1)S(1)}, bf16[512,1024]{1,0:T(8,128)(2,1)}, u32[]{:S(2)}) copy-start(bf16[512,1024]{1,0:T(8,128)(2,1)} %param.6) | copy-start | bytes 3145732

commit v2 on v1

--- a/solution.py
+++ b/solution.py
@@ -27,7 +27,7 @@
     n_pts, n_cen, codes_ref, cen_ref, out_ref, pen_ref,
     allc, stat, norm, weighted, counts, own_sq,
     recv, half, stat_recv, norm_recv,
-    send_z, send_x, send_c, send_core, send_hx, send_hc, send_stat, send_norm, own_sem,
+    send_up, send_down, send_x, send_c, send_core, send_hx, send_hc, send_stat, send_norm, own_sem,
 ):
     n, width = codes_ref.shape
     n_z = n_pts // 4
@@ -56,11 +56,8 @@
             device_id=peer, device_id_type=MESH,
         )
 
-    sent = []
-
     def push(copy):
         copy.start()
-        sent.append(copy)
 
     def whole(b, send_sem, peer, src=None):
         push(remote(allc.at[b] if src is None else src, allc.at[b], send_sem, recv.at[b], peer))
@@ -75,6 +72,64 @@
     def part_arrived(b, h):
         rows = pl.ds(h * (n // 2), n // 2)
         remote(allc.at[b, rows], allc.at[b, rows], own_sem, half.at[b, h], core_peer).wait_recv()
+
+    has_up, has_down = z < n_z - 1, z > 0
+    up_peer = (pts_of(lax.rem(z + 1, n_z), x, core), c)
+    down_peer = (pts_of(lax.rem(z + n_z - 1, n_z), x, core), c)
+
+    def at_distance(d, visit):
+        if d == 0:
+            visit(z)
+            return
+
+        @pl.when(z + d < n_z)
+        def _():
+            visit(z + d)
+
+        @pl.when(z >= d)
+        def _():
+            visit(z - d)
+
+    def fan_out(zi, src=None):
+        b = block(zi, x, core, c)
+
+        @pl.when(jnp.logical_and(has_up, zi <= z))
+        def _():
+            whole(b, send_up.at[zi], up_peer, src)
+
+        @pl.when(jnp.logical_and(has_down, zi >= z))
+        def _():
+            whole(b, send_down.at[zi], down_peer, src)
+
+        for j in range(1, n_cen):
+            whole(b, send_c.at[zi, j], (p, c_at(j)), src)
+        whole(b, send_x.at[zi], x_peer, src)
+        whole(b, send_core.at[zi, 0, 0], core_peer, src)
+
+    def from_line(zi):
+        arrived(block(zi, x, core, c))
+        fan_out(zi)
+
+    def from_cen(zi):
+        for j in range(1, n_cen):
+            b = block(zi, x, core, c_at(j))
+            arrived(b)
+            part(b, 1, send_hx.at[zi, j], x_peer)
+            whole(b, send_core.at[zi, 0, j], core_peer)
+
+    def from_x(zi):
+        b = block(zi, 1 - x, core, c)
+        arrived(b)
+        for j in range(1, n_cen):
+            part(b, 0, send_hc.at[zi, j], (p, c_at(j)))
+        whole(b, send_core.at[zi, 1, 0], core_peer)
+
+    def from_both(zi):
+        for j in range(1, n_cen):
+            b = block(zi, 1 - x, core, c_at(j))
+            part_arrived(b, 0)
+            part_arrived(b, 1)
+            whole(b, send_core.at[zi, 1, j], core_peer)
 
     barrier = pltpu.get_barrier_semaphore()
     for k in range(1, n_pts):
@@ -87,34 +142,14 @@
 
     own = pltpu.make_async_copy(codes_ref, allc.at[mine], own_sem)
     own.start()
-    for j in range(1, n_cen):
-        whole(mine, send_c.at[0, j], (p, c_at(j)), codes_ref)
-    for k in range(1, n_z):
-        whole(mine, send_z.at[k], (pts_of(z_at(k), x, core), c), codes_ref)
-    whole(mine, send_x.at[0], x_peer, codes_ref)
-    whole(mine, send_core.at[0, 0, 0], core_peer, codes_ref)
+    fan_out(z, codes_ref)
     own.wait()
 
     owned = out_ref.shape[0]
     own_rows = pl.ds(pl.multiple_of(p * owned, owned), owned)
     own_sq[...] = scaled_squares(cen_ref[0, own_rows, :])
 
-    for k in range(1, n_z):
-        b = block(z_at(k), x, core, c)
-        arrived(b)
-        whole(b, send_x.at[k], x_peer)
-        for j in range(1, n_cen):
-            whole(b, send_c.at[k, j], (p, c_at(j)))
-        whole(b, send_core.at[k, 0, 0], core_peer)
-
-    def from_cen(k):
-        for j in range(1, n_cen):
-            b = block(z_at(k), x, core, c_at(j))
-            arrived(b)
-            part(b, 1, send_hx.at[k, j], x_peer)
-            whole(b, send_core.at[k, 0, j], core_peer)
-
-    from_cen(0)
+    from_cen(z)
 
     tile = min(256, cen_ref.shape[1])
     group_rows = n * n_cen
@@ -132,30 +167,29 @@
         )
         return peak_next, total_next
 
-    peak, total = lax.fori_loop(
-        0,
-        cen_ref.shape[1] // tile,
-        stats_step,
-        (
-            jnp.full((1, group_rows), -jnp.inf, jnp.float32),
-            jnp.zeros((1, group_rows), jnp.float32),
-        ),
+    tiles = cen_ref.shape[1] // tile
+    stats = (
+        jnp.full((1, group_rows), -jnp.inf, jnp.float32),
+        jnp.zeros((1, group_rows), jnp.float32),
     )
+    for d in range(1, n_z + 1):
+        lo, hi = tiles * (d - 1) // n_z, tiles * d // n_z
+        stats = lax.fori_loop(lo, hi, stats_step, stats)
+        if d < n_z:
+            at_distance(d, from_line)
+            at_distance(d - 1, from_x)
+            if d > 1:
+                at_distance(d - 1, from_cen)
+    peak, total = stats
     first = lax.broadcasted_iota(jnp.int32, (8, n), 0) == 0
     for j in range(n_cen):
         cols = slice(j * n, (j + 1) * n)
         stat[c, j] = jnp.where(first, peak[:, cols], total[:, cols])
     for j in range(1, n_cen):
         push(remote(stat.at[c], stat.at[c], send_stat.at[j], stat_recv.at[c], (p, c_at(j))))
-
-    for k in range(n_z):
-        b = block(z_at(k), 1 - x, core, c)
-        arrived(b)
-        for j in range(1, n_cen):
-            part(b, 0, send_hc.at[k, j], (p, c_at(j)))
-        whole(b, send_core.at[k, 1, 0], core_peer)
-        if k > 0:
-            from_cen(k)
+    at_distance(n_z - 1, from_x)
+    if n_z > 1:
+        at_distance(n_z - 1, from_cen)
 
     for j in range(1, n_cen):
         s = c_at(j)
@@ -168,7 +202,7 @@
         for s in range(n_cen):
             piece = stat[s, j]
             mass = mass + piece[1:2, :] * jnp.exp(piece[0:1, :] - top)
-        norm[p, j] = jnp.broadcast_to(top + jnp.log(mass), (8, n))
+        norm[p, :, j * n:(j + 1) * n] = jnp.broadcast_to(top + jnp.log(mass), (8, n))
     for k in range(1, n_pts):
         push(
             remote(
@@ -182,15 +216,8 @@
         preferred_element_type=jnp.float32, precision=lax.Precision.HIGHEST,
     )
     pen_ref[...] = (-(smoothing_scale / width)) * (
-        norm[p, c][0:1, :] - lengths[0:1, :] / smoothing_scale
+        norm[p, 0:1, pl.ds(pl.multiple_of(c * n, n), n)] - lengths[0:1, :] / smoothing_scale
     )
-
-    for k in range(n_z):
-        for j in range(1, n_cen):
-            b = block(z_at(k), 1 - x, core, c_at(j))
-            part_arrived(b, 0)
-            part_arrived(b, 1)
-            whole(b, send_core.at[k, 1, j], core_peer)
 
     for k in range(1, n_pts):
         s = lax.rem(p + k, n_pts)
@@ -199,38 +226,74 @@
     weighted[...] = jnp.zeros_like(weighted)
     counts[...] = jnp.zeros_like(counts)
 
-    def consume(zi, xi, ki, ci):
-        rows = allc[block(zi, xi, ki, ci)]
+    def consume(pi):
+        rows = allc[pl.ds(pi * n_cen, n_cen)].reshape(group_rows, width)
         scores = lax.dot_general(
             cen_ref[0, own_rows, :], rows, NT, preferred_element_type=jnp.float32
         )
-        shift = norm[pts_of(zi, xi, ki), ci][0:1, :]
-        resp = jnp.exp(scores * (2.0 / smoothing_scale) - own_sq[...] - shift)
+        resp = jnp.exp(scores * (2.0 / smoothing_scale) - own_sq[...] - norm[pi, 0:1, :])
         lanes = resp[:, 0:128]
-        for q in range(1, n // 128):
+        for q in range(1, group_rows // 128):
             lanes = lanes + resp[:, q * 128:(q + 1) * 128]
         counts[...] += lanes
         weighted[...] += jnp.dot(
             resp.astype(jnp.bfloat16), rows, preferred_element_type=jnp.float32
         )
 
-    def same_core(i, _):
-        consume(i // (2 * n_cen), lax.rem(i // n_cen, 2), core, lax.rem(i, n_cen))
+    def line(i, _):
+        from_both(z_at(i))
+        consume(pts_of(z_at(i), x, core))
         return 0
 
+    def across(i, _):
+        consume(pts_of(z_at(i), 1 - x, core))
+        return 0
+
     def other_core(i, _):
-        zi, xi, ci = i // (2 * n_cen), lax.rem(i // n_cen, 2), lax.rem(i, n_cen)
-        arrived(block(zi, xi, 1 - core, ci))
-        consume(zi, xi, 1 - core, ci)
+        zi, xi = z_at(lax.rem(i, n_z)), lax.rem(x + i // n_z, 2)
+        for ci in range(n_cen):
+            arrived(block(zi, xi, 1 - core, ci))
+        consume(pts_of(zi, xi, 1 - core))
         return 0
 
-    lax.fori_loop(0, n_z * 2 * n_cen, same_core, 0)
-    lax.fori_loop(0, n_z * 2 * n_cen, other_core, 0)
+    lax.fori_loop(0, n_z, line, 0)
+    lax.fori_loop(0, n_z, across, 0)
+    lax.fori_loop(0, 2 * n_z, other_core, 0)
 
     tally = jnp.sum(counts[...], axis=1, keepdims=True)
     out_ref[...] = (weighted[...] + cen_ref[0, own_rows, :].astype(jnp.float32)) / (tally + 1.0)
-    for copy in sent:
-        copy.wait_send()
+
+    def left(ref, send_sem):
+        remote(ref, ref, send_sem, own_sem, core_peer).wait_send()
+
+    block_ref, half_ref = allc.at[0], allc.at[0, pl.ds(0, n // 2)]
+    for zi in range(n_z):
+
+        @pl.when(jnp.logical_and(has_up, zi <= z))
+        def _():
+            left(block_ref, send_up.at[zi])
+
+        @pl.when(jnp.logical_and(has_down, zi >= z))
+        def _():
+            left(block_ref, send_down.at[zi])
+
+        left(block_ref, send_x.at[zi])
+        for j in range(n_cen):
+            left(block_ref, send_core.at[zi, 0, j])
+            left(block_ref, send_core.at[zi, 1, j])
+            if j > 0:
+                left(block_ref, send_c.at[zi, j])
+                left(half_ref, send_hx.at[zi, j])
+                left(half_ref, send_hc.at[zi, j])
+    for j in range(1, n_cen):
+        left(stat.at[0], send_stat.at[j])
+    for k in range(1, n_pts):
+        left(norm.at[0], send_norm.at[k])
+
+
+def finish(fresh_ref, pen_ref, out_ref, cost_ref):
+    out_ref[0] = fresh_ref[...]
+    cost_ref[...] = pen_ref[0]
 
 
 def body(n_pts, n_cen, states, first_weight, first_bias, second_weight, centroids):
@@ -250,7 +313,7 @@
         scratch_shapes=[
             pltpu.VMEM((n_pts * n_cen, n, width), jnp.bfloat16),
             pltpu.VMEM((n_cen, n_cen, 8, n), jnp.float32),
-            pltpu.VMEM((n_pts, n_cen, 8, n), jnp.float32),
+            pltpu.VMEM((n_pts, 8, n_cen * n), jnp.float32),
             pltpu.VMEM((owned, width), jnp.float32),
             pltpu.VMEM((owned, 128), jnp.float32),
             pltpu.VMEM((owned, 1), jnp.float32),
@@ -258,6 +321,7 @@
             dma((n_pts * n_cen, 2)),
             dma((n_cen,)),
             dma((n_pts,)),
+            dma((n_z,)),
             dma((n_z,)),
             dma((n_z,)),
             dma((n_z, n_cen)),
@@ -272,7 +336,15 @@
             collective_id=0, has_side_effects=True, vmem_limit_bytes=60 * 1024 * 1024
         ),
     )(codes, centroids)
-    return (fresh[None], penalty.reshape(n))
+    return pl.pallas_call(
+        finish,
+        out_shape=(
+            jax.ShapeDtypeStruct((1, owned, width), jnp.float32),
+            jax.ShapeDtypeStruct((n,), jnp.float32),
+        ),
+        in_specs=[pl.BlockSpec(memory_space=pltpu.VMEM)] * 2,
+        out_specs=(pl.BlockSpec(memory_space=pltpu.VMEM),) * 2,
+    )(fresh, penalty)
 
 
 def solution(mesh):

time: 59.1 us -> 50.5 us (0.85)
  the two profiles are of different devices: /device:TPU:13 before, /device:TPU:0 now
where the time goes in v2:
time: 50.5 us; the launch traced here: 50.3 us
  Pallas kernels  45.9 us (91%)
  matrix products  2.56 us (5%)
  local copies, waits for them, and re-layouts  1.22 us (2%)
  between operations  0.65 us (1%)
    pallas_call x1, Pallas kernels, body(): pl.pallas_call(functools.partial(kernel, n_pts, n_cen), out_shape=(jax.Sh...  44.2 us
    dot_general x1, matrix products, encode(): jnp.dot(hidden, second_weight, preferred_element_type=jnp.float32)  2.56 us
    pallas_call x1, Pallas kernels, body(): pl.pallas_call(finish, out_shape=(jax.ShapeDtypeStruct((1, owned, width),...  1.68 us
    unnamed x2, local copies, waits for them, and re-layouts  1.22 us

profile of v2, /device:TPU:0, one launch (start us, length us, event | category | flops | bytes accessed | tf_op | source)
XLA Modules:
  0.0 50.3 jit_solution(6068575712692557906)
XLA Ops:
  0.6 0.0 copy-start
  0.6 1.2 %copy-done = bf16[512,1024]{1,0:T(8,128)(2,1)S(1)} copy-done((bf16[512,1024]{1,0:T(8,128)(2,1)S(1)}, bf16[512,1024]{1,0:T(8,128)(2,1)}, u32[]{:S(2)}) %copy-start) | copy-done | bytes 1048600
  1.9 2.6 %convolution_convert_fusion.codes_ref = bf16[256,256]{1,0:T(8,128)(2,1)} fusion(bf16[1024,256]{1,0:T(8,128)(2,1)} %param.8, bf16[256,512]{1,0:T(8,128)(2,1)} %param.5, bf16[512,1024]{1,0:T(8,128)(2,1)S(1)} %copy-done, f32[1024]{0:T(1024)} %param.7), kind=kOutput, calls=%fused_computation.2 | convolution fusion | flops 405340160 | bytes 1970176 | tf_op jit(solution)/shard_map/dot_general | solution.py:18
  4.4 44.2 %shard_map.68 = (f32[256,256]{1,0:T(8,128)}, f32[1,256]{1,0:T(1,128)}) custom-call(bf16[256,256]{1,0:T(8,128)(2,1)} %convolution_convert_fusion.codes_ref, bf16[1,4096,256]{2,1,0:T(8,128)(2,1)} %cen_ref.1), custom_call_target="tpu_custom_call" | custom-call | tf_op jit(solution)/shard_map/pallas_call | solution.py:305
  48.6 1.7 %shard_map.69 = (f32[1,256,256]{2,1,0:T(8,128)}, f32[256]{0:T(256)}) custom-call(f32[256,256]{1,0:T(8,128)} %get-tuple-element.4.fresh_ref, f32[1,256]{1,0:T(1,128)} %get-tuple-element.5.pen_ref), custom_call_target="tpu_custom_call" | custom-call | tf_op jit(solution)/shard_map/pallas_call | solution.py:339
Async XLA Ops:
  0.6 1.2 %copy-start = (bf16[512,1024]{1,0:T(8,128)(2,1)S(1)}, bf16[512,1024]{1,0:T(8,128)(2,1)}, u32[]{:S(2)}) copy-start(bf16[512,1024]{1,0:T(8,128)(2,1)} %param.6) | copy-start | bytes 3145732

commit v3 on v2

--- a/solution.py
+++ b/solution.py
@@ -12,24 +12,32 @@
 NT = (((1,), (1,)), ((), ()))
 
 
-def encode(states, first_weight, first_bias, second_weight):
-    pre = jnp.dot(states, first_weight, preferred_element_type=jnp.float32) + first_bias
-    hidden = jax.nn.gelu(pre).astype(jnp.bfloat16)
-    return jnp.dot(hidden, second_weight, preferred_element_type=jnp.float32).astype(jnp.bfloat16)
-
-
 def scaled_squares(rows):
     wide = rows.astype(jnp.float32)
     return jnp.sum(wide * wide, axis=1, keepdims=True) / smoothing_scale
 
 
 def kernel(
-    n_pts, n_cen, codes_ref, cen_ref, out_ref, pen_ref,
+    n_pts, n_cen, states_hbm, first_hbm, bias_ref, second_hbm, cen_hbm, out_ref, pen_ref,
+    states_ref, first_ref, second_ref, cen_ref, load_sem,
     allc, stat, norm, weighted, counts, own_sq,
     recv, half, stat_recv, norm_recv,
     send_up, send_down, send_x, send_c, send_core, send_hx, send_hc, send_stat, send_norm, own_sem,
 ):
-    n, width = codes_ref.shape
+    n, width = states_ref.shape[0], second_ref.shape[1]
+    loads = [
+        pltpu.make_async_copy(src, dst, load_sem.at[i])
+        for i, (src, dst) in enumerate(
+            (
+                (states_hbm, states_ref),
+                (first_hbm, first_ref),
+                (second_hbm, second_ref),
+                (cen_hbm.at[0], cen_ref),
+            )
+        )
+    ]
+    for load in loads:
+        load.start()
     n_z = n_pts // 4
     p, c = lax.axis_index("pts"), lax.axis_index("cen")
     core, x, z = lax.rem(p, 2), lax.rem(p // 2, 2), p // 4
@@ -59,8 +67,8 @@
     def push(copy):
         copy.start()
 
-    def whole(b, send_sem, peer, src=None):
-        push(remote(allc.at[b] if src is None else src, allc.at[b], send_sem, recv.at[b], peer))
+    def whole(b, send_sem, peer):
+        push(remote(allc.at[b], allc.at[b], send_sem, recv.at[b], peer))
 
     def part(b, h, send_sem, peer):
         rows = pl.ds(h * (n // 2), n // 2)
@@ -90,21 +98,21 @@
         def _():
             visit(z - d)
 
-    def fan_out(zi, src=None):
+    def fan_out(zi):
         b = block(zi, x, core, c)
 
         @pl.when(jnp.logical_and(has_up, zi <= z))
         def _():
-            whole(b, send_up.at[zi], up_peer, src)
+            whole(b, send_up.at[zi], up_peer)
 
         @pl.when(jnp.logical_and(has_down, zi >= z))
         def _():
-            whole(b, send_down.at[zi], down_peer, src)
+            whole(b, send_down.at[zi], down_peer)
 
         for j in range(1, n_cen):
-            whole(b, send_c.at[zi, j], (p, c_at(j)), src)
-        whole(b, send_x.at[zi], x_peer, src)
-        whole(b, send_core.at[zi, 0, 0], core_peer, src)
+            whole(b, send_c.at[zi, j], (p, c_at(j)))
+        whole(b, send_x.at[zi], x_peer)
+        whole(b, send_core.at[zi, 0, 0], core_peer)
 
     def from_line(zi):
         arrived(block(zi, x, core, c))
@@ -138,26 +146,30 @@
         )
     for j in range(1, n_cen):
         pl.semaphore_signal(barrier, inc=1, device_id=(p, c_at(j)), device_id_type=MESH)
-    pl.semaphore_wait(barrier, n_pts - 1 + n_cen - 1)
-
-    own = pltpu.make_async_copy(codes_ref, allc.at[mine], own_sem)
-    own.start()
-    fan_out(z, codes_ref)
-    own.wait()
-
+    loads[0].wait()
+    loads[1].wait()
+    pre = jnp.dot(states_ref[...], first_ref[...], preferred_element_type=jnp.float32)
+    hidden = jax.nn.gelu(pre + bias_ref[...][None, :]).astype(jnp.bfloat16)
+    loads[2].wait()
+    allc[mine] = jnp.dot(
+        hidden, second_ref[...], preferred_element_type=jnp.float32
+    ).astype(jnp.bfloat16)
+    loads[3].wait()
     owned = out_ref.shape[0]
     own_rows = pl.ds(pl.multiple_of(p * owned, owned), owned)
-    own_sq[...] = scaled_squares(cen_ref[0, own_rows, :])
+    own_sq[...] = scaled_squares(cen_ref[own_rows, :])
+    pl.semaphore_wait(barrier, n_pts - 1 + n_cen - 1)
+    fan_out(z)
 
     from_cen(z)
 
-    tile = min(256, cen_ref.shape[1])
+    tile = min(512, cen_ref.shape[0])
     group_rows = n * n_cen
     group = pl.ds(p * n_cen, n_cen)
 
     def stats_step(i, carry):
         peak, total = carry
-        centers = cen_ref[0, pl.ds(pl.multiple_of(i * tile, tile), tile), :]
+        centers = cen_ref[pl.ds(pl.multiple_of(i * tile, tile), tile), :]
         rows = allc[group].reshape(group_rows, width)
         scores = lax.dot_general(centers, rows, NT, preferred_element_type=jnp.float32)
         scores = scores * (2.0 / smoothing_scale) - scaled_squares(centers)
@@ -167,7 +179,7 @@
         )
         return peak_next, total_next
 
-    tiles = cen_ref.shape[1] // tile
+    tiles = cen_ref.shape[0] // tile
     stats = (
         jnp.full((1, group_rows), -jnp.inf, jnp.float32),
         jnp.zeros((1, group_rows), jnp.float32),
@@ -210,7 +222,7 @@
                 (lax.rem(p + k, n_pts), c),
             )
         )
-    wide = codes_ref[...].astype(jnp.float32)
+    wide = allc[mine].astype(jnp.float32)
     lengths = lax.dot_general(
         jnp.ones((8, width), jnp.float32), wide * wide, NT,
         preferred_element_type=jnp.float32, precision=lax.Precision.HIGHEST,
@@ -229,7 +241,7 @@
     def consume(pi):
         rows = allc[pl.ds(pi * n_cen, n_cen)].reshape(group_rows, width)
         scores = lax.dot_general(
-            cen_ref[0, own_rows, :], rows, NT, preferred_element_type=jnp.float32
+            cen_ref[own_rows, :], rows, NT, preferred_element_type=jnp.float32
         )
         resp = jnp.exp(scores * (2.0 / smoothing_scale) - own_sq[...] - norm[pi, 0:1, :])
         lanes = resp[:, 0:128]
@@ -256,12 +268,12 @@
         consume(pts_of(zi, xi, 1 - core))
         return 0
 
-    lax.fori_loop(0, n_z, line, 0)
-    lax.fori_loop(0, n_z, across, 0)
-    lax.fori_loop(0, 2 * n_z, other_core, 0)
+    lax.fori_loop(0, n_z, line, 0, unroll=n_z <= 4)
+    lax.fori_loop(0, n_z, across, 0, unroll=n_z <= 4)
+    lax.fori_loop(0, 2 * n_z, other_core, 0, unroll=n_z <= 4)
 
     tally = jnp.sum(counts[...], axis=1, keepdims=True)
-    out_ref[...] = (weighted[...] + cen_ref[0, own_rows, :].astype(jnp.float32)) / (tally + 1.0)
+    out_ref[...] = (weighted[...] + cen_ref[own_rows, :].astype(jnp.float32)) / (tally + 1.0)
 
     def left(ref, send_sem):
         remote(ref, ref, send_sem, own_sem, core_peer).wait_send()
@@ -297,8 +309,7 @@
 
 
 def body(n_pts, n_cen, states, first_weight, first_bias, second_weight, centroids):
-    codes = encode(states, first_weight, first_bias, second_weight)
-    n, width = codes.shape
+    n, width = states.shape[0], second_weight.shape[1]
     owned = centroids.shape[1] // n_pts
     n_z = n_pts // 4
     dma = pltpu.SemaphoreType.DMA
@@ -308,9 +319,20 @@
             jax.ShapeDtypeStruct((owned, width), jnp.float32),
             jax.ShapeDtypeStruct((1, n), jnp.float32),
         ),
-        in_specs=[pl.BlockSpec(memory_space=pltpu.VMEM)] * 2,
+        in_specs=[
+            pl.BlockSpec(memory_space=pl.ANY),
+            pl.BlockSpec(memory_space=pl.ANY),
+            pl.BlockSpec(memory_space=pltpu.VMEM),
+            pl.BlockSpec(memory_space=pl.ANY),
+            pl.BlockSpec(memory_space=pl.ANY),
+        ],
         out_specs=(pl.BlockSpec(memory_space=pltpu.VMEM),) * 2,
         scratch_shapes=[
+            pltpu.VMEM(states.shape, states.dtype),
+            pltpu.VMEM(first_weight.shape, first_weight.dtype),
+            pltpu.VMEM(second_weight.shape, second_weight.dtype),
+            pltpu.VMEM(centroids.shape[1:], centroids.dtype),
+            dma((4,)),
             pltpu.VMEM((n_pts * n_cen, n, width), jnp.bfloat16),
             pltpu.VMEM((n_cen, n_cen, 8, n), jnp.float32),
             pltpu.VMEM((n_pts, 8, n_cen * n), jnp.float32),
@@ -335,7 +357,7 @@
         compiler_params=pltpu.CompilerParams(
             collective_id=0, has_side_effects=True, vmem_limit_bytes=60 * 1024 * 1024
         ),
-    )(codes, centroids)
+    )(states, first_weight, first_bias, second_weight, centroids)
     return pl.pallas_call(
         finish,
         out_shape=(

time: 50.5 us -> 42.7 us (0.85)
  Pallas kernels: 45.9 us -> 41.8 us
  matrix products: 2.56 us -> 0 us
  local copies, waits for them, and re-layouts: 1.22 us -> 0 us
    pallas_call x1, Pallas kernels: 44.2 us -> 40.2 us  [body(): pl.pallas_call(functools.partial(kernel, n_pts, n_cen), out_shape=(jax.Sh...]
    dot_general x1 -> x0, matrix products: 2.56 us -> none  [encode(): jnp.dot(hidden, second_weight, preferred_element_type=jnp.float32)]
    unnamed x2 -> x0, local copies, waits for them, and re-layouts: 1.22 us -> none
where the time goes in v3:
time: 42.7 us; the launch traced here: 42.5 us
  Pallas kernels  41.8 us (98%)
  between operations  0.64 us (1%)
    pallas_call x1, Pallas kernels, body(): pl.pallas_call(functools.partial(kernel, n_pts, n_cen), out_shape=(jax.Sh...  40.2 us
    pallas_call x1, Pallas kernels, body(): pl.pallas_call(finish, out_shape=(jax.ShapeDtypeStruct((1, owned, width),...  1.68 us

profile of v3, /device:TPU:0, one launch (start us, length us, event | category | flops | bytes accessed | tf_op | source)
XLA Modules:
  0.0 42.5 jit_solution(10754697411719536816)
XLA Ops:
  0.6 40.2 %shard_map.68 = (f32[256,256]{1,0:T(8,128)}, f32[1,256]{1,0:T(1,128)}) custom-call(bf16[256,512]{1,0:T(8,128)(2,1)} %states_hbm.1, bf16[512,1024]{1,0:T(8,128)(2,1)} %first_hbm.1, f32[1024]{0:T(1024)} %bias_ref.1, bf16[1024,256]{1,0:T(8,128)(2,1)} %second_hbm.1, bf16[1,4096,256]{2,1,0:T(8,128)(2,1)} %cen_hbm.1), custom_call_target="tpu_custom_call" | custom-call | tf_op jit(solution)/shard_map/pallas_call | solution.py:316
  40.8 1.7 %shard_map.69 = (f32[1,256,256]{2,1,0:T(8,128)}, f32[256]{0:T(256)}) custom-call(f32[256,256]{1,0:T(8,128)} %get-tuple-element.4.fresh_ref, f32[1,256]{1,0:T(1,128)} %get-tuple-element.5.pen_ref), custom_call_target="tpu_custom_call" | custom-call | tf_op jit(solution)/shard_map/pallas_call | solution.py:361
